TPU v7x, 1024 devices: a whole 8x8x8 slice. The times are simulated.
1024 devices in a mesh: dir: 32 (over z, x_lo), slab: 32 (over y, x_hi, core).
Axes of the slice: x: 8 (x_hi: 2, x_lo: 4; x = x_hi * 4 + x_lo), y: 8, z: 8, core: 2. Of those that a mesh axis runs over, the one named last changes fastest.
Arguments:
- child_fields: bfloat16 [64, 32, 2, 8, 2, 2, 512], P('slab', 'dir'), may hold values from -6 to 6
- occupancy: int32 [64, 32, 2], P('slab', 'dir'), may hold values 0 or 1
- child_octant: int32 [64, 32, 2, 8], P('slab', 'dir'), may hold values from 0 to 7, each once within a row
- shift_angle: float32 [8, 2048], replicated, may hold values from -3.140625 to 3.140625
- interp_matrix: bfloat16 [512, 2048], replicated, may hold values from -0.25 to 0.25
- trans_table: float32 [7, 7, 7, 2, 2048], P(None, None, None, None, 'dir'), may hold values from -0.2 to 0.2
- impedance: float32 [64, 32, 2, 8, 2], P('slab', 'dir'), may hold values from -4 to 4
Outputs:
- child_incoming: bfloat16 [64, 32, 2, 8, 2, 2, 512], P('slab', 'dir')
Inputs may be any that keep to these rules, and one draw needn't show every extreme that they name: `child_octant`: the 8 child slots of every parent box name the 8 octants once each.
All inputs are finite; a program needn't handle non-finite values. No bound on the sum of `occupancy` on one device may be relied on, other than what follows from the above.
Results may differ from a plain program's by a relative error of at most 0.0064.
Values may be sent and summed in bfloat16 or wider, within the bound.
A program may use at most 128 MiB of HBM per device.

v0:
```python
import functools

import jax
import jax.numpy as jnp
from jax import lax
from jax.experimental import pallas as pl
from jax.experimental.pallas import tpu as pltpu
from jax.sharding import PartitionSpec as P

MESH = pl.DeviceIdType.MESH
F32 = jnp.float32
BF16 = jnp.bfloat16


def lane_low(shape):
    return lax.broadcasted_iota(jnp.int32, shape, 1) < 64


def fused(
    n_dir, n_slab, scale,
    x_ref, occ_ref, oct_ref, ang_hbm, interp_hbm, table_hbm, imp_ref,
    out_ref,
    ang, interp, table, cos_t, sin_t, select, selectf, imp_cols, spread, send1, recv1,
    factors, field, totals, flat, send2, recv2, split,
    local_sem, send1_sem, recv1_sem, send2_sem, recv2_sem,
):
    d = lax.axis_index("dir")
    s = lax.axis_index("slab")
    not_first = s > 0
    not_last = s < n_slab - 1

    barrier = pltpu.get_barrier_semaphore()

    @pl.loop(0, n_dir)
    def _(k):
        t = lax.rem(d + k, n_dir)

        @pl.when(not_first)
        def _():
            pl.semaphore_signal(barrier, inc=1, device_id={"dir": t, "slab": s - 1}, device_id_type=MESH)

        @pl.when(not_last)
        def _():
            pl.semaphore_signal(barrier, inc=1, device_id={"dir": t, "slab": s + 1}, device_id_type=MESH)

        @pl.when(k > 0)
        def _():
            pl.semaphore_signal(barrier, inc=1, device_id={"dir": t, "slab": s}, device_id_type=MESH)

    load_ang = pltpu.make_async_copy(ang_hbm, ang, local_sem.at[0])
    load_interp = pltpu.make_async_copy(interp_hbm, interp, local_sem.at[1])
    load_table = pltpu.make_async_copy(table_hbm.at[:, :, 2:5], table, local_sem.at[2])
    load_ang.start()
    load_interp.start()
    load_table.start()

    lane = lax.broadcasted_iota(jnp.int32, (1, 128), 1)
    oct_lane = jnp.zeros((1, 128), jnp.int32)
    occ_lane = jnp.zeros((1, 128), F32)
    imp_re = jnp.zeros((1, 128), F32)
    imp_im = jnp.zeros((1, 128), F32)
    for box in range(4):
        x, z = box // 2, box % 2
        occ_lane = jnp.where(lane // 32 == box, occ_ref[x, 0, z].astype(F32), occ_lane)
        for slot in range(8):
            here = lane // 4 == box * 8 + slot
            oct_lane = jnp.where(here, oct_ref[x, 0, z, slot], oct_lane)
            imp_re = jnp.where(here, imp_ref[x, 0, z, slot, 0], imp_re)
            imp_im = jnp.where(here, imp_ref[x, 0, z, slot, 1], imp_im)
    row16 = lax.broadcasted_iota(jnp.int32, (16, 128), 0)
    lane16 = lax.broadcasted_iota(jnp.int32, (16, 128), 1)
    same = (row16 // 8 == (lane16 // 2) % 2) & ((row16 // 4) % 2 == lane16 % 2) & (row16 % 4 == lane16 // 32)
    for q in range(8):
        picked = jnp.where(same & (oct_lane == q), 1.0, 0.0).astype(F32)
        selectf[q * 16 : q * 16 + 16, :] = picked
        select[q * 16 : q * 16 + 16, :] = (picked * occ_lane).astype(BF16)
        imp_cols[0, q * 16 : q * 16 + 16, :] = jnp.broadcast_to(jnp.sum(picked * imp_re, axis=1, keepdims=True), (16, 128))
        imp_cols[1, q * 16 : q * 16 + 16, :] = jnp.broadcast_to(jnp.sum(picked * imp_im, axis=1, keepdims=True), (16, 128))

    sorted_x = jnp.dot(select[...], x_ref[...], preferred_element_type=F32).astype(BF16)
    load_ang.wait()
    cos_t[...] = jnp.cos(ang[...])
    sin_t[...] = jnp.sin(ang[...])
    load_interp.wait()
    spread[...] = jnp.dot(sorted_x, interp[...], preferred_element_type=F32)

    low8 = lane_low((8, 128))
    real8 = lax.broadcasted_iota(jnp.int32, (8, 128), 0) < 4
    up_sign = jnp.where(real8, -1.0, 1.0).astype(F32)
    down_sign = jnp.where(real8, 1.0, -1.0).astype(F32)

    @pl.loop(0, n_dir // 2)
    def _(j):
        cols = pl.ds(pl.multiple_of(j * 128, 128), 128)
        parts = []
        for e in range(2):
            straight = jnp.zeros((8, 128), F32)
            crossed = jnp.zeros((8, 128), F32)
            for q in range(8):
                v = spread[q * 16 + e * 8 : q * 16 + e * 8 + 8, cols]
                straight += cos_t[q : q + 1, cols] * v
                crossed += sin_t[q : q + 1, cols] * v
            parts.append(straight + up_sign * pltpu.roll(crossed, 4, 0))
        e0, e1 = parts
        send1[2 * j] = jnp.where(low8, e0, pltpu.roll(e1, 64, 1)).astype(BF16)
        send1[2 * j + 1] = jnp.where(low8, pltpu.roll(e0, 64, 1), e1).astype(BF16)

    pl.semaphore_wait(
        barrier,
        n_dir - 1 + n_dir * not_first.astype(jnp.int32) + n_dir * not_last.astype(jnp.int32),
    )

    @pl.loop(0, n_dir)
    def _(k):
        t = lax.rem(d + k, n_dir)

        @pl.when(not_first)
        def _():
            pltpu.make_async_remote_copy(
                send1.at[t], recv1.at[2, d], send1_sem.at[0], recv1_sem.at[2],
                device_id={"dir": t, "slab": s - 1}, device_id_type=MESH,
            ).start()

        @pl.when(not_last)
        def _():
            pltpu.make_async_remote_copy(
                send1.at[t], recv1.at[0, d], send1_sem.at[2], recv1_sem.at[0],
                device_id={"dir": t, "slab": s + 1}, device_id_type=MESH,
            ).start()

        @pl.when(k > 0)
        def _():
            pltpu.make_async_remote_copy(
                send1.at[t], recv1.at[1, d], send1_sem.at[1], recv1_sem.at[1],
                device_id={"dir": t, "slab": s}, device_id_type=MESH,
            ).start()

    pltpu.make_async_copy(send1.at[d], recv1.at[1, d], recv1_sem.at[1]).start()

    load_table.wait()

    @pl.loop(0, 49)
    def _(i):
        a, b = i // 7, i % 7
        for c in range(3):
            for part in range(2):
                row = table[a, b, c, part : part + 1, :]
                both = jnp.concatenate([row, row], axis=1)
                factors[i * 6 + c * 2 + part] = jnp.broadcast_to(both, (8, 128))

    field[0:16, :] = jnp.zeros((16, 128), F32)
    field[16 + 8 * n_dir :, :] = jnp.zeros((16, 128), F32)
    totals[...] = jnp.zeros_like(totals)

    def gather_slab(k):
        pltpu.make_async_copy(recv1.at[k], recv1.at[k], recv1_sem.at[k]).wait()
        field[16 : 16 + 8 * n_dir, :] = recv1[k].astype(F32).reshape(8 * n_dir, 128)

        @pl.loop(0, n_dir // 16)
        def _(h):
            acc = [totals[h, i] for i in range(16)]
            for xl in range(2):
                p = 2 * k + xl
                for y in range(6):
                    for z in range(2):
                        rows = [
                            pl.ds((16 * h + y) * 8 + part * 4 + xl * 2 + z, 8, stride=16) for part in range(2)
                        ]
                        targets = [
                            (px, py, pz)
                            for px in range(2) for py in range(2) for pz in range(2)
                            if max(abs(p - 2 - px), abs(y - 2 - py)) > 1
                        ]
                        if not targets:
                            continue
                        re, im = field[rows[0], :], field[rows[1], :]
                        for px, py, pz in targets:
                            at = ((p + 1 - px) * 7 + y + 1 - py) * 6 + (z - pz + 1) * 2
                            fr, fi = factors[at], factors[at + 1]
                            i = (px * 2 + pz) * 2 + py
                            acc[i] = acc[i] + fr * re - fi * im
                            acc[8 + i] = acc[8 + i] + fr * im + fi * re
            for i in range(16):
                totals[h, i] = acc[i]

    gather_slab(1)

    @pl.when(not_first)
    def _():
        gather_slab(0)

    @pl.when(not_last)
    def _():
        gather_slab(2)

    @pl.loop(0, n_dir // 16)
    def _(h):
        for part in range(2):
            for px in range(2):
                for pz in range(2):
                    for py in range(2):
                        row = (16 * h + py) * 8 + part * 4 + px * 2 + pz
                        flat[pl.ds(row, 8, stride=16), :] = totals[h, part * 8 + (px * 2 + pz) * 2 + py]

    send2[...] = flat[...].reshape(n_dir, 8, 128).astype(BF16)

    @pl.loop(1, n_dir)
    def _(k):
        t = lax.rem(d + k, n_dir)
        pltpu.make_async_remote_copy(
            send2.at[t], recv2.at[d], send2_sem, recv2_sem,
            device_id={"dir": t, "slab": s}, device_id_type=MESH,
        ).start()

    pltpu.make_async_copy(send2.at[d], recv2.at[d], recv2_sem).start()
    unsort = selectf[...].T.astype(BF16)
    pltpu.make_async_copy(recv2, recv2, recv2_sem).wait()

    @pl.loop(0, n_dir // 2)
    def _(j):
        cols = pl.ds(pl.multiple_of(j * 128, 128), 128)
        a = recv2[2 * j].astype(F32)
        b = recv2[2 * j + 1].astype(F32)
        e0 = jnp.where(low8, a, pltpu.roll(b, 64, 1))
        e1 = jnp.where(low8, pltpu.roll(a, 64, 1), b)
        x0 = down_sign * pltpu.roll(e0, 4, 0)
        x1 = down_sign * pltpu.roll(e1, 4, 0)
        for q in range(8):
            c, n = cos_t[q : q + 1, cols], sin_t[q : q + 1, cols]
            both = jnp.concatenate([c * e0 + n * x0, c * e1 + n * x1], axis=0)
            split[q * 16 : q * 16 + 16, cols] = both.astype(BF16)

    gathered = scale * lax.dot_general(
        split[...], interp[...], (((1,), (1,)), ((), ())), preferred_element_type=F32
    )
    width = gathered.shape[1]
    blocks = gathered.reshape(16, 8, width)
    swapped = jnp.concatenate([-blocks[:, 4:], blocks[:, :4]], axis=1).reshape(128, width)
    scaled = imp_cols[0, :, 0:1] * gathered + imp_cols[1, :, 0:1] * swapped
    out_ref[...] = jnp.dot(unsort, scaled.astype(BF16), preferred_element_type=F32).astype(BF16)

    pltpu.make_async_copy(send1.at[0 : n_dir - 1], send1.at[0 : n_dir - 1], send1_sem.at[1]).wait()
    pltpu.make_async_copy(send2.at[0 : n_dir - 1], send2.at[0 : n_dir - 1], send2_sem).wait()

    @pl.when(not_first)
    def _():
        pltpu.make_async_copy(send1, send1, send1_sem.at[0]).wait()

    @pl.when(not_last)
    def _():
        pltpu.make_async_copy(send1, send1, send1_sem.at[2]).wait()


def body(child_fields, occupancy, child_octant, shift_angle, interp_matrix, trans_table, impedance):
    n_dir, n_slab = lax.axis_size("dir"), lax.axis_size("slab")
    kc, kp = interp_matrix.shape
    scale = (kc / kp) ** 0.5
    vmem = pl.BlockSpec(memory_space=pltpu.VMEM)
    smem = pl.BlockSpec(memory_space=pltpu.SMEM)
    anywhere = pl.BlockSpec(memory_space=pl.ANY)
    rows = child_fields.reshape(-1, kc)
    out = pl.pallas_call(
        functools.partial(fused, n_dir, n_slab, scale),
        out_shape=jax.ShapeDtypeStruct(rows.shape, BF16),
        in_specs=[vmem, smem, smem, anywhere, anywhere, anywhere, smem],
        out_specs=vmem,
        scratch_shapes=[
            pltpu.VMEM((8, kp), F32),
            pltpu.VMEM((kc, kp), BF16),
            pltpu.VMEM((7, 7, 3, 2, 64), F32),
            pltpu.VMEM((8, kp), F32),
            pltpu.VMEM((8, kp), F32),
            pltpu.VMEM((128, 128), BF16),
            pltpu.VMEM((128, 128), F32),
            pltpu.VMEM((2, 128, 128), F32),
            pltpu.VMEM((128, kp), F32),
            pltpu.VMEM((n_dir, 8, 128), BF16),
            pltpu.VMEM((3, n_dir, 8, 128), BF16),
            pltpu.VMEM((294, 8, 128), F32),
            pltpu.VMEM((8 * n_dir + 32, 128), F32),
            pltpu.VMEM((n_dir // 16, 16, 8, 128), F32),
            pltpu.VMEM((8 * n_dir, 128), F32),
            pltpu.VMEM((n_dir, 8, 128), BF16),
            pltpu.VMEM((n_dir, 8, 128), BF16),
            pltpu.VMEM((128, kp), BF16),
            pltpu.SemaphoreType.DMA((3,)),
            pltpu.SemaphoreType.DMA((3,)),
            pltpu.SemaphoreType.DMA((3,)),
            pltpu.SemaphoreType.DMA,
            pltpu.SemaphoreType.DMA,
        ],
        compiler_params=pltpu.CompilerParams(collective_id=0, has_side_effects=True),
    )(rows, occupancy, child_octant, shift_angle, interp_matrix, trans_table, impedance)
    return out.reshape(child_fields.shape)


def solution(mesh):
    placed = (
        P("slab", "dir", None, None, None, None, None),
        P("slab", "dir", None),
        P("slab", "dir", None, None),
        P(),
        P(),
        P(None, None, None, None, "dir"),
        P("slab", "dir", None, None, None),
    )
    return jax.shard_map(
        body,
        mesh=mesh,
        in_specs=placed,
        out_specs=P("slab", "dir", None, None, None, None, None),
        check_vma=False,
    )
```

profile of v0, /device:TPU:80, one launch (start us, length us, event | category | flops | bytes accessed | tf_op | source)
XLA Modules:
  0.0 46.4 jit_solution(12864488858025821846)
XLA Ops:
  0.0 1.4 %copy.8.imp_ref = f32[2,1,2,8,2]{4,3,2,1,0:T(8,128)} copy(f32[2,1,2,8,2]{3,4,2,1,0:T(2,128)} %param.13) | data formatting | bytes 512 | tf_op args[6]
  1.4 1.6 %reshape.6.x_ref = bf16[128,512]{1,0:T(8,128)(2,1)} reshape(bf16[2,1,2,8,2,2,512]{6,5,4,3,2,1,0:T(2,128)(2,1)} %param.7) | data formatting | bytes 262144 | tf_op jit(solution)/shard_map/reshape | solution.py:261
  3.0 41.8 %shard_map.73 = bf16[128,512]{1,0:T(8,128)(2,1)} custom-call(bf16[128,512]{1,0:T(8,128)(2,1)} %reshape.6.x_ref, s32[2,1,2]{2,1,0:T(1,128)} %occ_ref.1, s32[2,1,2,8]{3,2,1,0:T(2,128)} %oct_ref.1, f32[8,2048]{1,0:T(8,128)} %ang_hbm.1, bf16[512,2048]{1,0:T(8,128)(2,1)} %interp_hbm.1, f32[7,7,7,2,64]{4,3,2,1,0:T(2,128)} %table_hbm.1, f32[2,1,2,8,2]{4,3,2,1,0:T(8,128)} %copy.8.imp_ref), custom_call_target="tpu_custom_call" | custom-call | tf_op jit(solution)/shard_map/pallas_call | solution.py:262
  44.8 1.6 %reshape.7 = bf16[2,1,2,8,2,2,512]{6,5,4,3,2,0,1:T(2,128)(2,1)} reshape(bf16[128,512]{1,0:T(8,128)(2,1)} %shard_map.73) | data formatting | bytes 262144 | tf_op jit(solution)/shard_map/reshape | solution.py:294
where the time goes:
time: 46.7 us; the launch traced here: 46.4 us
  Pallas kernels  41.8 us (90%)
  local copies, waits for them, and re-layouts  4.6 us (10%)
    pallas_call x1, Pallas kernels, body(): pl.pallas_call(functools.partial(fused, n_dir, n_slab, scale), out_shape=...  41.8 us
    reshape x1, local copies, waits for them, and re-layouts, body(): return out.reshape(child_fields.shape)  1.62 us
    reshape x1, local copies, waits for them, and re-layouts, body(): rows = child_fields.reshape(-1, kc)  1.61 us
    unnamed x1, local copies, waits for them, and re-layouts  1.37 us

commit v1 on v0

v1 whole, which is shorter than its diff:
```python
import functools

import jax
import jax.numpy as jnp
from jax import lax
from jax.experimental import pallas as pl
from jax.experimental.pallas import tpu as pltpu
from jax.sharding import PartitionSpec as P

MESH = pl.DeviceIdType.MESH
F32 = jnp.float32
BF16 = jnp.bfloat16


def lane_low(shape):
    return lax.broadcasted_iota(jnp.int32, shape, 1) < 64

PLANES = 8
UNTIL = (0, 3, 5, 8)


def fused(
    n_dir, n_slab, scale,
    x_hbm, occ_hbm, oct_hbm, ang_hbm, interp_hbm, table_hbm, imp_hbm,
    out_ref,
    x_in, occ_ref, oct_ref, imp_ref, ang, interp, table, cos_t, sin_t, selectf, imp_cols, spread, send1, recv1,
    real_of, imag_of, field, flat, send2, recv2, split,
    local_sem, send1_sem, recv1_sem, send2_sem, recv2_sem,
):
    d = lax.axis_index("dir")
    s = lax.axis_index("slab")
    not_first = s > 0
    not_last = s < n_slab - 1
    width = n_dir // PLANES
    plane = d // width
    half = n_dir // 2

    loads = [
        pltpu.make_async_copy(a, b, local_sem.at[i])
        for i, (a, b) in enumerate(
            [
                (x_hbm, x_in), (occ_hbm, occ_ref), (oct_hbm, oct_ref), (imp_hbm, imp_ref), (ang_hbm, ang),
                (interp_hbm, interp), (table_hbm.at[:, :, 2:5], table),
            ]
        )
    ]
    for load in loads:
        load.start()

    barrier = pltpu.get_barrier_semaphore()

    @pl.loop(0, n_dir)
    def _(k):
        i = k // width
        ahead = PLANES // 2 + i // 2 - (i % 2) * (1 + 2 * (i // 2))
        t = lax.rem(plane + ahead, PLANES) * width + lax.rem(k + d, width)

        @pl.when(not_first)
        def _():
            pl.semaphore_signal(barrier, inc=1, device_id={"dir": t, "slab": s - 1}, device_id_type=MESH)

        @pl.when(not_last)
        def _():
            pl.semaphore_signal(barrier, inc=1, device_id={"dir": t, "slab": s + 1}, device_id_type=MESH)

        @pl.when(t != d)
        def _():
            pl.semaphore_signal(barrier, inc=1, device_id={"dir": t, "slab": s}, device_id_type=MESH)

    low8 = lane_low((8, 128))
    real8 = lax.broadcasted_iota(jnp.int32, (8, 128), 0) < 4
    up_sign = jnp.where(real8, -1.0, 1.0).astype(F32)
    down_sign = jnp.where(real8, 1.0, -1.0).astype(F32)

    for load in loads[:5]:
        load.wait()
    cos_t[...] = jnp.cos(ang[...])
    sin_t[...] = jnp.sin(ang[...])
    lane = lax.broadcasted_iota(jnp.int32, (1, 128), 1)
    oct_lane = jnp.zeros((1, 128), jnp.int32)
    occ_lane = jnp.zeros((1, 128), F32)
    for box in range(4):
        x, z = box // 2, box % 2
        occ_lane = jnp.where(lane // 32 == box, occ_ref[x, 0, z].astype(F32), occ_lane)
        for slot in range(8):
            oct_lane = jnp.where(lane // 4 == box * 8 + slot, oct_ref[x, 0, z, slot], oct_lane)
    row16 = lax.broadcasted_iota(jnp.int32, (16, 128), 0)
    lane16 = lax.broadcasted_iota(jnp.int32, (16, 128), 1)
    same = (row16 // 8 == (lane16 // 2) % 2) & ((row16 // 4) % 2 == lane16 % 2) & (row16 % 4 == lane16 // 32)
    picked = [jnp.where(same & (oct_lane == q), 1.0, 0.0).astype(F32) for q in range(8)]
    for q in range(8):
        selectf[q * 16 : q * 16 + 16, :] = picked[q]
    select = jnp.concatenate([(p * occ_lane).astype(BF16) for p in picked], axis=0)
    rows_in = x_in[...].reshape(128, x_in.shape[2])
    sorted_x = jnp.dot(select, rows_in, preferred_element_type=F32).astype(BF16)
    loads[5].wait()

    spread[...] = jnp.dot(sorted_x, interp[...], preferred_element_type=F32)

    @pl.loop(0, n_dir // 2, unroll=4)
    def _(j):
        cols = pl.ds(pl.multiple_of(j * 128, 128), 128)
        parts = []
        for e in range(2):
            straight = jnp.zeros((8, 128), F32)
            crossed = jnp.zeros((8, 128), F32)
            for q in range(8):
                v = spread[q * 16 + e * 8 : q * 16 + e * 8 + 8, cols]
                straight += cos_t[q : q + 1, cols] * v
                crossed += sin_t[q : q + 1, cols] * v
            parts.append(straight + up_sign * pltpu.roll(crossed, 4, 0))
        e0, e1 = parts
        send1[2 * j] = jnp.where(low8, e0, pltpu.roll(e1, 64, 1)).astype(BF16)
        send1[2 * j + 1] = jnp.where(low8, pltpu.roll(e0, 64, 1), e1).astype(BF16)

    pl.semaphore_wait(
        barrier, n_dir - 1 + n_dir * (not_first.astype(jnp.int32) + not_last.astype(jnp.int32))
    )

    part = (plane >= UNTIL[1]).astype(jnp.int32) + (plane >= UNTIL[2]).astype(jnp.int32)

    @pl.loop(0, n_dir)
    def _(k):
        t = (PLANES - 1 - k // width) * width + lax.rem(k + d, width)

        @pl.when(not_first)
        def _():
            pltpu.make_async_remote_copy(
                send1.at[t], recv1.at[2, d], send1_sem.at[0], recv1_sem.at[2, part],
                device_id={"dir": t, "slab": s - 1}, device_id_type=MESH,
            ).start()

        @pl.when(not_last)
        def _():
            pltpu.make_async_remote_copy(
                send1.at[t], recv1.at[0, d], send1_sem.at[2], recv1_sem.at[0, part],
                device_id={"dir": t, "slab": s + 1}, device_id_type=MESH,
            ).start()

        @pl.when(t != d)
        def _():
            pltpu.make_async_remote_copy(
                send1.at[t], recv1.at[1, d], send1_sem.at[1], recv1_sem.at[1, part],
                device_id={"dir": t, "slab": s}, device_id_type=MESH,
            ).start()

        @pl.when(t == d)
        def _():
            pltpu.make_async_copy(send1.at[t], recv1.at[1, d], recv1_sem.at[1, part]).start()

    loads[6].wait()
    for a in range(7):
        rows = table[a].reshape(21, 2, 64)
        re, im = rows[:, 0, :], rows[:, 1, :]
        real_of[21 * a : 21 * a + 21, :] = jnp.concatenate([re, re], axis=1)
        imag_of[21 * a : 21 * a + 21, :] = jnp.concatenate([im, im], axis=1)

    imp_re = jnp.zeros((1, 128), F32)
    imp_im = jnp.zeros((1, 128), F32)
    for box in range(4):
        x, z = box // 2, box % 2
        for slot in range(8):
            here = lane // 4 == box * 8 + slot
            imp_re = jnp.where(here, imp_ref[x, 0, z, 0, slot], imp_re)
            imp_im = jnp.where(here, imp_ref[x, 0, z, 1, slot], imp_im)
    for q in range(8):
        row = selectf[q * 16 : q * 16 + 16, :]
        imp_cols[0, q * 16 : q * 16 + 16, :] = jnp.broadcast_to(jnp.sum(row * imp_re, axis=1, keepdims=True), (16, 128))
        imp_cols[1, q * 16 : q * 16 + 16, :] = jnp.broadcast_to(jnp.sum(row * imp_im, axis=1, keepdims=True), (16, 128))
    unsort = selectf[...].T.astype(BF16)

    for k in range(3):
        field[k, 0:16, :] = jnp.zeros((16, 128), F32)
        field[k, 16 + 8 * n_dir :, :] = jnp.zeros((16, 128), F32)

    @pl.when(jnp.logical_not(not_first))
    def _():
        field[0] = jnp.zeros(field.shape[1:], F32)

    @pl.when(jnp.logical_not(not_last))
    def _():
        field[2] = jnp.zeros(field.shape[1:], F32)

    middle = 8 * (UNTIL[2] - UNTIL[1]) * width
    for k in range(3):
        field[k, 16 + 8 * UNTIL[1] * width : 16 + 8 * UNTIL[1] * width + middle, :] = jnp.zeros((middle, 128), F32)

    def arrive(k, item):
        first, count = UNTIL[item] * width, (UNTIL[item + 1] - UNTIL[item]) * width
        block = recv1.at[k, first : first + count]
        pltpu.make_async_copy(block, block, recv1_sem.at[k, item]).wait()
        field[k, 16 + 8 * first : 16 + 8 * (first + count), :] = block[...].astype(F32).reshape(8 * count, 128)

    @pl.loop(0, 3)
    def _(item):
        for i in range(3):
            @pl.when(item == i)
            def _(i=i):
                arrive(1, i)

                @pl.when(not_first)
                def _():
                    arrive(0, i)

                @pl.when(not_last)
                def _():
                    arrive(2, i)

        h = item // 2
        acc = [jnp.zeros((8, 128), F32) for _ in range(16)]
        for p in range(6):
            k, xl = p // 2, p % 2
            for y in range(6):
                for z in range(2):
                    targets = [
                        (px, py, pz)
                        for px in range(2) for py in range(2) for pz in range(2)
                        if max(abs(p - 2 - px), abs(y - 2 - py)) > 1
                    ]
                    if not targets:
                        continue
                    re, im = [
                        field[k, pl.ds((half * h + y) * 8 + c * 4 + xl * 2 + z, 8, stride=16), :] for c in range(2)
                    ]
                    for px, py, pz in targets:
                        at = ((p + 1 - px) * 7 + y + 1 - py) * 3 + z - pz + 1
                        fr, fi = real_of[at : at + 1, :], imag_of[at : at + 1, :]
                        i = (px * 2 + pz) * 2 + py
                        acc[i] = acc[i] + fr * re - fi * im
                        acc[8 + i] = acc[8 + i] + fr * im + fi * re
        for c in range(2):
            for px in range(2):
                for pz in range(2):
                    for py in range(2):
                        row = py * 8 + c * 4 + px * 2 + pz
                        flat[pl.ds(row, 8, stride=16), :] = acc[c * 8 + (px * 2 + pz) * 2 + py]
        quarter = n_dir // 4

        @pl.when(item < 2)
        def _():
            boxes = flat[pl.ds(pl.multiple_of(item * 8 * quarter, 8 * quarter), 8 * quarter), :]
            send2[pl.ds(item * quarter, quarter)] = boxes.reshape(quarter, 8, 128).astype(BF16)

        @pl.when(item == 2)
        def _():
            send2[half:] = flat[...].reshape(half, 8, 128).astype(BF16)

        @pl.loop(0, quarter * (1 + h))
        def _(k):
            t = item * quarter + (k // width) * width + lax.rem(k + d, width)

            @pl.when(t != d)
            def _():
                pltpu.make_async_remote_copy(
                    send2.at[t], recv2.at[d], send2_sem, recv2_sem,
                    device_id={"dir": t, "slab": s}, device_id_type=MESH,
                ).start()

            @pl.when(t == d)
            def _():
                pltpu.make_async_copy(send2.at[t], recv2.at[d], recv2_sem).start()

    pltpu.make_async_copy(recv2, recv2, recv2_sem).wait()

    @pl.loop(0, n_dir // 2, unroll=4)
    def _(j):
        cols = pl.ds(pl.multiple_of(j * 128, 128), 128)
        a = recv2[2 * j].astype(F32)
        b = recv2[2 * j + 1].astype(F32)
        e0 = jnp.where(low8, a, pltpu.roll(b, 64, 1))
        e1 = jnp.where(low8, pltpu.roll(a, 64, 1), b)
        x0 = down_sign * pltpu.roll(e0, 4, 0)
        x1 = down_sign * pltpu.roll(e1, 4, 0)
        for q in range(8):
            c, n = cos_t[q : q + 1, cols], sin_t[q : q + 1, cols]
            both = jnp.concatenate([c * e0 + n * x0, c * e1 + n * x1], axis=0)
            split[q * 16 : q * 16 + 16, cols] = both.astype(BF16)

    gathered = scale * lax.dot_general(
        split[...], interp[...], (((1,), (1,)), ((), ())), preferred_element_type=F32
    )
    across_k = gathered.shape[1]
    blocks = gathered.reshape(16, 8, across_k)
    swapped = jnp.concatenate([-blocks[:, 4:], blocks[:, :4]], axis=1).reshape(128, across_k)
    scaled = imp_cols[0, :, 0:1] * gathered + imp_cols[1, :, 0:1] * swapped
    out_ref[...] = jnp.dot(unsort, scaled.astype(BF16), preferred_element_type=F32).astype(BF16)

    pltpu.make_async_copy(send1.at[0 : n_dir - 1], send1.at[0 : n_dir - 1], send1_sem.at[1]).wait()
    pltpu.make_async_copy(send2.at[0 : n_dir - 1], send2.at[0 : n_dir - 1], send2_sem).wait()

    @pl.when(not_first)
    def _():
        pltpu.make_async_copy(send1, send1, send1_sem.at[0]).wait()

    @pl.when(not_last)
    def _():
        pltpu.make_async_copy(send1, send1, send1_sem.at[2]).wait()


def body(child_fields, occupancy, child_octant, shift_angle, interp_matrix, trans_table, impedance):
    n_dir, n_slab = lax.axis_size("dir"), lax.axis_size("slab")
    kc, kp = interp_matrix.shape
    scale = (kc / kp) ** 0.5
    anywhere = pl.BlockSpec(memory_space=pl.ANY)
    pairs = child_fields.reshape(-1, 2, kc)
    by_part = jnp.swapaxes(impedance, 3, 4)
    out = pl.pallas_call(
        functools.partial(fused, n_dir, n_slab, scale),
        out_shape=jax.ShapeDtypeStruct((2 * pairs.shape[0], kc), BF16),
        in_specs=[anywhere] * 7,
        out_specs=pl.BlockSpec(memory_space=pltpu.VMEM),
        scratch_shapes=[
            pltpu.VMEM(pairs.shape, BF16),
            pltpu.SMEM(occupancy.shape, jnp.int32),
            pltpu.SMEM(child_octant.shape, jnp.int32),
            pltpu.SMEM(by_part.shape, F32),
            pltpu.VMEM((8, kp), F32),
            pltpu.VMEM((kc, kp), BF16),
            pltpu.VMEM((7, 7, 3, 2, 64), F32),
            pltpu.VMEM((8, kp), F32),
            pltpu.VMEM((8, kp), F32),
            pltpu.VMEM((128, 128), F32),
            pltpu.VMEM((2, 128, 128), F32),
            pltpu.VMEM((128, kp), F32),
            pltpu.VMEM((n_dir, 8, 128), BF16),
            pltpu.VMEM((3, n_dir, 8, 128), BF16),
            pltpu.VMEM((152, 128), F32),
            pltpu.VMEM((152, 128), F32),
            pltpu.VMEM((3, 8 * n_dir + 32, 128), F32),
            pltpu.VMEM((4 * n_dir, 128), F32),
            pltpu.VMEM((n_dir, 8, 128), BF16),
            pltpu.VMEM((n_dir, 8, 128), BF16),
            pltpu.VMEM((128, kp), BF16),
            pltpu.SemaphoreType.DMA((7,)),
            pltpu.SemaphoreType.DMA((3,)),
            pltpu.SemaphoreType.DMA((3, 3)),
            pltpu.SemaphoreType.DMA,
            pltpu.SemaphoreType.DMA,
        ],
        compiler_params=pltpu.CompilerParams(collective_id=0, has_side_effects=True),
    )(pairs, occupancy, child_octant, shift_angle, interp_matrix, trans_table, by_part)
    return out.reshape(child_fields.shape)


def solution(mesh):
    placed = (
        P("slab", "dir", None, None, None, None, None),
        P("slab", "dir", None),
        P("slab", "dir", None, None),
        P(),
        P(),
        P(None, None, None, None, "dir"),
        P("slab", "dir", None, None, None),
    )
    return jax.shard_map(
        body,
        mesh=mesh,
        in_specs=placed,
        out_specs=P("slab", "dir", None, None, None, None, None),
        check_vma=False,
    )
```

time: 46.7 us -> 41.3 us (0.88)
  the two profiles are of different devices: /device:TPU:80 before, /device:TPU:64 now
where the time goes in v1:
time: 41.3 us; the launch traced here: 41.2 us
  Pallas kernels  39.5 us (96%)
  local copies, waits for them, and re-layouts  1.62 us (4%)
    pallas_call x1, Pallas kernels, body(): pl.pallas_call(functools.partial(fused, n_dir, n_slab, scale), out_shape=...  39.5 us
    reshape x1, local copies, waits for them, and re-layouts, body(): return out.reshape(child_fields.shape)  1.62 us

profile of v1, /device:TPU:64, one launch (start us, length us, event | category | flops | bytes accessed | tf_op | source)
XLA Modules:
  0.0 41.2 jit_solution(12933311323385671194)
XLA Ops:
  0.0 39.5 %shard_map.73 = bf16[128,512]{1,0:T(8,128)(2,1)} custom-call(bf16[64,2,512]{2,1,0:T(2,128)(2,1)} %bitcast.3, s32[2,1,2]{2,1,0:T(1,128)} %occ_hbm.1, s32[2,1,2,8]{3,2,1,0:T(2,128)} %oct_hbm.1, f32[8,2048]{1,0:T(8,128)} %ang_hbm.1, bf16[512,2048]{1,0:T(8,128)(2,1)} %interp_hbm.1, f32[7,7,7,2,64]{4,3,2,1,0:T(2,128)} %table_hbm.1, f32[2,1,2,2,8]{4,3,2,1,0:T(2,128)} %bitcast.4), custom_call_target="tpu_custom_call" | custom-call | tf_op jit(solution)/shard_map/pallas_call | solution.py:307
  39.5 1.6 %reshape.7 = bf16[2,1,2,8,2,2,512]{6,5,4,3,2,0,1:T(2,128)(2,1)} reshape(bf16[128,512]{1,0:T(8,128)(2,1)} %shard_map.73) | data formatting | bytes 262144 | tf_op jit(solution)/shard_map/reshape | solution.py:342

commit v2 on v1

--- a/solution.py
+++ b/solution.py
@@ -24,7 +24,7 @@
     x_hbm, occ_hbm, oct_hbm, ang_hbm, interp_hbm, table_hbm, imp_hbm,
     out_ref,
     x_in, occ_ref, oct_ref, imp_ref, ang, interp, table, cos_t, sin_t, selectf, imp_cols, spread, send1, recv1,
-    real_of, imag_of, field, flat, send2, recv2, split,
+    real_of, imag_of, field, flat, send2, recv2, split, partial_sum,
     local_sem, send1_sem, recv1_sem, send2_sem, recv2_sem,
 ):
     d = lax.axis_index("dir")
@@ -252,33 +252,39 @@
             @pl.when(t != d)
             def _():
                 pltpu.make_async_remote_copy(
-                    send2.at[t], recv2.at[d], send2_sem, recv2_sem,
+                    send2.at[t], recv2.at[d], send2_sem, recv2_sem.at[d // half],
                     device_id={"dir": t, "slab": s}, device_id_type=MESH,
                 ).start()
 
             @pl.when(t == d)
             def _():
-                pltpu.make_async_copy(send2.at[t], recv2.at[d], recv2_sem).start()
-
-    pltpu.make_async_copy(recv2, recv2, recv2_sem).wait()
-
-    @pl.loop(0, n_dir // 2, unroll=4)
-    def _(j):
-        cols = pl.ds(pl.multiple_of(j * 128, 128), 128)
-        a = recv2[2 * j].astype(F32)
-        b = recv2[2 * j + 1].astype(F32)
-        e0 = jnp.where(low8, a, pltpu.roll(b, 64, 1))
-        e1 = jnp.where(low8, pltpu.roll(a, 64, 1), b)
-        x0 = down_sign * pltpu.roll(e0, 4, 0)
-        x1 = down_sign * pltpu.roll(e1, 4, 0)
-        for q in range(8):
-            c, n = cos_t[q : q + 1, cols], sin_t[q : q + 1, cols]
-            both = jnp.concatenate([c * e0 + n * x0, c * e1 + n * x1], axis=0)
-            split[q * 16 : q * 16 + 16, cols] = both.astype(BF16)
-
-    gathered = scale * lax.dot_general(
-        split[...], interp[...], (((1,), (1,)), ((), ())), preferred_element_type=F32
-    )
+                pltpu.make_async_copy(send2.at[t], recv2.at[d], recv2_sem.at[d // half]).start()
+
+    def half_back(part):
+        replies = recv2.at[half * part : half * part + half]
+        pltpu.make_async_copy(replies, replies, recv2_sem.at[part]).wait()
+
+        @pl.loop(part * (half // 2), (part + 1) * (half // 2), unroll=4)
+        def _(j):
+            cols = pl.ds(pl.multiple_of(j * 128, 128), 128)
+            a = recv2[2 * j].astype(F32)
+            b = recv2[2 * j + 1].astype(F32)
+            e0 = jnp.where(low8, a, pltpu.roll(b, 64, 1))
+            e1 = jnp.where(low8, pltpu.roll(a, 64, 1), b)
+            x0 = down_sign * pltpu.roll(e0, 4, 0)
+            x1 = down_sign * pltpu.roll(e1, 4, 0)
+            for q in range(8):
+                c, n = cos_t[q : q + 1, cols], sin_t[q : q + 1, cols]
+                both = jnp.concatenate([c * e0 + n * x0, c * e1 + n * x1], axis=0)
+                split[q * 16 : q * 16 + 16, cols] = both.astype(BF16)
+
+        columns = slice(64 * half * part, 64 * half * (part + 1))
+        return lax.dot_general(
+            split[:, columns], interp[:, columns], (((1,), (1,)), ((), ())), preferred_element_type=F32
+        )
+
+    partial_sum[...] = half_back(0)
+    gathered = scale * (partial_sum[...] + half_back(1))
     across_k = gathered.shape[1]
     blocks = gathered.reshape(16, 8, across_k)
     swapped = jnp.concatenate([-blocks[:, 4:], blocks[:, :4]], axis=1).reshape(128, across_k)
@@ -306,7 +312,7 @@
     by_part = jnp.swapaxes(impedance, 3, 4)
     out = pl.pallas_call(
         functools.partial(fused, n_dir, n_slab, scale),
-        out_shape=jax.ShapeDtypeStruct((2 * pairs.shape[0], kc), BF16),
+        out_shape=pltpu.VMEM((2 * pairs.shape[0], kc), BF16),
         in_specs=[anywhere] * 7,
         out_specs=pl.BlockSpec(memory_space=pltpu.VMEM),
         scratch_shapes=[
@@ -331,11 +337,12 @@
             pltpu.VMEM((n_dir, 8, 128), BF16),
             pltpu.VMEM((n_dir, 8, 128), BF16),
             pltpu.VMEM((128, kp), BF16),
+            pltpu.VMEM((128, kc), F32),
             pltpu.SemaphoreType.DMA((7,)),
             pltpu.SemaphoreType.DMA((3,)),
             pltpu.SemaphoreType.DMA((3, 3)),
             pltpu.SemaphoreType.DMA,
-            pltpu.SemaphoreType.DMA,
+            pltpu.SemaphoreType.DMA((2,)),
         ],
         compiler_params=pltpu.CompilerParams(collective_id=0, has_side_effects=True),
     )(pairs, occupancy, child_octant, shift_angle, interp_matrix, trans_table, by_part)

time: 41.3 us -> 39.2 us (0.949)
  Pallas kernels: 39.5 us -> 38.3 us
  local copies, waits for them, and re-layouts: 1.62 us -> 0.71 us
    pallas_call x1, Pallas kernels: 39.5 us -> 38.3 us  [body(): pl.pallas_call(functools.partial(fused, n_dir, n_slab, scale), out_shape=...]
    reshape x1, local copies, waits for them, and re-layouts: 1.62 us -> 0.71 us  [body(): return out.reshape(child_fields.shape)]
where the time goes in v2:
time: 39.2 us; the launch traced here: 39 us
  Pallas kernels  38.3 us (98%)
  local copies, waits for them, and re-layouts  0.71 us (2%)
    pallas_call x1, Pallas kernels, body(): pl.pallas_call(functools.partial(fused, n_dir, n_slab, scale), out_shape=...  38.3 us

profile of v2, /device:TPU:64, one launch (start us, length us, event | category | flops | bytes accessed | tf_op | source)
XLA Modules:
  0.0 39.0 jit_solution(17251594271723470103)
XLA Ops:
  0.0 38.3 %shard_map.73 = bf16[128,512]{1,0:T(8,128)(2,1)S(1)} custom-call(bf16[64,2,512]{2,1,0:T(2,128)(2,1)} %bitcast.3, s32[2,1,2]{2,1,0:T(1,128)} %occ_hbm.1, s32[2,1,2,8]{3,2,1,0:T(2,128)} %oct_hbm.1, f32[8,2048]{1,0:T(8,128)} %ang_hbm.1, bf16[512,2048]{1,0:T(8,128)(2,1)} %interp_hbm.1, f32[7,7,7,2,64]{4,3,2,1,0:T(2,128)} %table_hbm.1, f32[2,1,2,2,8]{4,3,2,1,0:T(2,128)} %bitcast.4), custom_call_target="tpu_custom_call" | custom-call | tf_op jit(solution)/shard_map/pallas_call | solution.py:313
  38.3 0.7 %reshape.7 = bf16[2,1,2,8,2,2,512]{6,5,4,3,2,0,1:T(2,128)(2,1)} reshape(bf16[128,512]{1,0:T(8,128)(2,1)S(1)} %shard_map.73) | data formatting | bytes 262144 | tf_op jit(solution)/shard_map/reshape | solution.py:349

commit v3 on v2

--- a/solution.py
+++ b/solution.py
@@ -289,7 +289,8 @@
     blocks = gathered.reshape(16, 8, across_k)
     swapped = jnp.concatenate([-blocks[:, 4:], blocks[:, :4]], axis=1).reshape(128, across_k)
     scaled = imp_cols[0, :, 0:1] * gathered + imp_cols[1, :, 0:1] * swapped
-    out_ref[...] = jnp.dot(unsort, scaled.astype(BF16), preferred_element_type=F32).astype(BF16)
+    result = jnp.dot(unsort, scaled.astype(BF16), preferred_element_type=F32).astype(BF16)
+    out_ref[...] = result.reshape(out_ref.shape)
 
     pltpu.make_async_copy(send1.at[0 : n_dir - 1], send1.at[0 : n_dir - 1], send1_sem.at[1]).wait()
     pltpu.make_async_copy(send2.at[0 : n_dir - 1], send2.at[0 : n_dir - 1], send2_sem).wait()
@@ -312,7 +313,7 @@
     by_part = jnp.swapaxes(impedance, 3, 4)
     out = pl.pallas_call(
         functools.partial(fused, n_dir, n_slab, scale),
-        out_shape=pltpu.VMEM((2 * pairs.shape[0], kc), BF16),
+        out_shape=pltpu.VMEM(pairs.shape, BF16),
         in_specs=[anywhere] * 7,
         out_specs=pl.BlockSpec(memory_space=pltpu.VMEM),
         scratch_shapes=[

time: 39.2 us -> 39.1 us (level)
    reshape x1 -> x0, local copies, waits for them, and re-layouts: 0.71 us -> none  [body(): return out.reshape(child_fields.shape)]
    unnamed x0 -> x1, local copies, waits for them, and re-layouts: none -> 0.66 us
where the time goes in v3:
time: 39.1 us; the launch traced here: 39 us
  Pallas kernels  38.3 us (98%)
  local copies, waits for them, and re-layouts  0.66 us (2%)
    pallas_call x1, Pallas kernels, body(): pl.pallas_call(functools.partial(fused, n_dir, n_slab, scale), out_shape=...  38.3 us

profile of v3, /device:TPU:64, one launch (start us, length us, event | category | flops | bytes accessed | tf_op | source)
XLA Modules:
  0.0 39.0 jit_solution(713408317943905461)
XLA Ops:
  0.0 38.3 %shard_map.73 = bf16[64,2,512]{2,1,0:T(2,128)(2,1)S(1)} custom-call(bf16[64,2,512]{2,1,0:T(2,128)(2,1)} %bitcast.6, s32[2,1,2]{2,1,0:T(1,128)} %occ_hbm.1, s32[2,1,2,8]{3,2,1,0:T(2,128)} %oct_hbm.1, f32[8,2048]{1,0:T(8,128)} %ang_hbm.1, bf16[512,2048]{1,0:T(8,128)(2,1)} %interp_hbm.1, f32[7,7,7,2,64]{4,3,2,1,0:T(2,128)} %table_hbm.1, f32[2,1,2,2,8]{4,3,2,1,0:T(2,128)} %bitcast.7), custom_call_target="tpu_custom_call" | custom-call | tf_op jit(solution)/shard_map/pallas_call | solution.py:314
  38.3 0.7 %copy.10 = bf16[2,1,2,8,2,2,512]{6,5,4,3,2,1,0:T(2,128)(2,1)} copy(bf16[2,1,2,8,2,2,512]{6,5,4,3,2,1,0:T(2,128)(2,1)S(1)} %bitcast.5) | data formatting | bytes 262144
